TPU v7x, 32 devices: a whole 2x2x4 slice. The times are simulated.
32 devices in a mesh: band: 2 (over y), slab: 16 (over z, x, core).
Axes of the slice: x: 2, y: 2, z: 4, core: 2. Of those that a mesh axis runs over, the one named last changes fastest.
Arguments:
- own_orbitals: float32 [4, 128, 128, 128], P('band', 'slab'), may hold values from -6 to 6
- partners: float32 [8, 128, 128, 128], P('band', 'slab'), may hold values from -6 to 6
Outputs:
- own_field: float32 [4, 128, 128, 128], P('band', 'slab')
- partner_field: float32 [8, 128, 128, 128], P('band', 'slab')
All inputs are finite; a program needn't handle non-finite values.
Results may differ from a plain program's by a relative error of at most 0.0001.
Values sent between devices are 32-bit elements; how exact they have to be, the bound alone decides.
No kernel may reach another device: no remote copies, remote signals or barrier semaphores. Data moves between devices by JAX's collectives and lax.ppermute only.
A program may use at most 128 MiB of HBM per device.

v0:
```python
import functools
import math
import jax
import jax.numpy as jnp
import numpy as np
from jax import lax
from jax.sharding import PartitionSpec as P

STEPS = 2
coulomb_scale = 46.9 * 46.9 / math.pi
precision = lax.Precision.HIGH


def cas_table(length):
    half = length // 2
    angles = np.arange(half) * (2.0 * math.pi / length)
    first = (np.cos(angles) + np.sin(angles)).astype(np.float32)
    wave = np.concatenate([first, -first])
    positions = np.arange(length)
    return wave[positions[:, None] * positions[None, :] % length]


def apply_table(pattern, field, table):
    return jnp.einsum(pattern, field, table, precision=precision)


def frequency(positions, length):
    return jnp.where(positions < length // 2, positions, positions - length).astype(jnp.float32)


def coulomb(z_waves, y_waves, x_waves, cells):
    square = (
        z_waves[:, None, None] * z_waves[:, None, None]
        + y_waves[None, :, None] * y_waves[None, :, None]
        + x_waves[None, None, :] * x_waves[None, None, :]
    )
    return jnp.where(square > 0, coulomb_scale / float(cells) / jnp.maximum(square, 1.0), 0.0)


def band_shift(block, groups, distance):
    if distance % groups == 0:
        return block
    route = [((b + distance) % groups, b) for b in range(groups)]
    return lax.ppermute(block, "band", route)


def pencils(own, partners, groups, slabs):
    length = own.shape[3]
    own_count, part_count = (own.shape[0], partners.shape[0])
    table = jnp.asarray(cas_table(length))
    rows_y = length // slabs
    waves = frequency(lax.iota(jnp.int32, length), length)
    y_waves = frequency(lax.axis_index("slab") * rows_y + lax.iota(jnp.int32, rows_y), length)
    kernel = coulomb(waves, y_waves, waves, length**3)
    own_acc = jnp.zeros(own.shape, jnp.float32)
    part_acc = jnp.zeros(partners.shape, jnp.float32)
    for step_no in sorted(range(1, STEPS + 1), key=lambda s: s % groups != 0):
        bands = band_shift(own, groups, step_no)
        field = (bands[:, None] * partners[None]).reshape((-1,) + own.shape[1:])
        field = apply_table("pzyx,xk->pzyk", field, table)
        field = apply_table("pzyx,yk->pzkx", field, table)
        field = lax.all_to_all(field, "slab", split_axis=2, concat_axis=1, tiled=True)
        field = apply_table("pzyx,zk->pkyx", field, table) * kernel
        field = apply_table("pzyx,zk->pkyx", field, table)
        field = lax.all_to_all(field, "slab", split_axis=1, concat_axis=2, tiled=True)
        field = apply_table("pzyx,yk->pzkx", field, table)
        field = apply_table("pzyx,xk->pzyk", field, table)
        potential = field.reshape((own_count, part_count) + own.shape[1:])
        part_acc = part_acc + jnp.sum(potential * bands[:, None], axis=0)
        own_add = jnp.sum(potential * partners[None], axis=1)
        own_acc = own_acc + band_shift(own_add, groups, -step_no)
    return (own_acc, part_acc)


def solution(mesh):
    groups, slabs = (mesh.shape["band"], mesh.shape["slab"])
    spec = P("band", "slab", None, None)
    return jax.shard_map(
        functools.partial(pencils, groups=groups, slabs=slabs),
        mesh=mesh,
        in_specs=(spec, spec),
        out_specs=(spec, spec),
        check_vma=False,
    )
```

profile of v0, /device:TPU:14, one launch (start us, length us, event | category | flops | bytes accessed | tf_op | source)
XLA Modules:
  0.0 468.5 jit_solution(9830222730541804954)
XLA Ops:
  1.2 24.6 %collective-permute-done = f32[2,8,128,128]{3,2,1,0:T(8,128)S(1)} collective-permute-done((f32[2,8,128,128]{3,2,1,0:T(8,128)}, f32[2,8,128,128]{3,2,1,0:T(8,128)S(1)}, u32[]{:S(2)}, u32[]{:S(2)}) %collective-permute-start) | collective-permute-done | bytes 1048608 | tf_op jit(solution)/shard_map/ppermute | solution.py:44
  25.8 5.1 %broadcast_multiply_fusion.1 = (f32[2,4,8,128,128]{4,3,2,1,0:T(8,128)S(1)}, f32[2,4,8,128,128]{4,3,2,1,0:T(8,128)}) fusion(f32[4,8,128,128]{3,2,1,0:T(8,128)} %param.4, f32[2,8,128,128]{3,2,1,0:T(8,128)} %param.3, f32[2,8,128,128]{3,2,1,0:T(8,128)S(1)} %collective-permute-done), kind=kLoop, calls=%fused_computation.29 | loop fusion | flops 2097152 | bytes 12582912 | tf_op jit(solution)/shard_map/mul | solution.py:59
  30.9 1.9 fusion.26
  32.8 3.4 convolution_bitcast_fusion.1
  36.2 5.4 %copy.12 = f32[8,8,128,128]{3,1,0,2:T(8,128)} copy(f32[8,8,128,128]{2,3,1,0:T(8,128)} %convolution_bitcast_fusion.1) | data formatting | bytes 8388608 | tf_op jit(solution)/shard_map/pzyx,yk->pzkx/transpose | solution.py:24
  41.6 6.2 %all-to-all-start = ((f32[8,8,128,128]{3,1,0,2:T(8,128)}), f32[8,8,128,128]{3,1,0,2:T(8,128)}, u32[]{:S(2)}, u32[]{:S(2)}) async-start(f32[8,8,128,128]{3,1,0,2:T(8,128)} %copy.12), calls=%async_computation | async-start | bytes 8388608 | tf_op jit(solution)/shard_map/all_to_all | solution.py:62
  47.8 4.1 fusion.27
  51.9 3.4 convolution_bitcast_fusion
  55.3 5.4 %copy.21 = f32[8,8,128,128]{3,1,0,2:T(8,128)} copy(f32[8,8,128,128]{2,3,1,0:T(8,128)} %convolution_bitcast_fusion) | data formatting | bytes 8388608 | tf_op jit(solution)/shard_map/pzyx,yk->pzkx/transpose | solution.py:24
  60.7 79.4 %all-to-all-done = f32[8,8,128,128]{3,1,0,2:T(8,128)} async-done(((f32[8,8,128,128]{3,1,0,2:T(8,128)}), f32[8,8,128,128]{3,1,0,2:T(8,128)}, u32[]{:S(2)}, u32[]{:S(2)}) %all-to-all-start) | async-done | bytes 4194336 | tf_op jit(solution)/shard_map/all_to_all | solution.py:62
  140.1 5.1 %all-to-all-start.2 = ((f32[8,8,128,128]{3,1,0,2:T(8,128)}), f32[8,8,128,128]{3,1,0,2:T(8,128)}, u32[]{:S(2)}, u32[]{:S(2)}) async-start(f32[8,8,128,128]{3,1,0,2:T(8,128)} %copy.21), calls=%async_computation.2 | async-start | bytes 8388608 | tf_op jit(solution)/shard_map/all_to_all | solution.py:62
  145.5 4.7 copy.13
  150.1 3.4 fusion.14
  153.6 3.4 fusion.16
  157.0 5.4 %copy.15 = f32[8,128,8,128]{3,2,0,1:T(8,128)} copy(f32[8,128,8,128]{1,3,2,0:T(8,128)} %fusion.16) | data formatting | bytes 8388608 | tf_op jit(solution)/shard_map/pzyx,zk->pkyx/transpose | solution.py:24
  162.4 75.1 %all-to-all-done.2 = f32[8,8,128,128]{3,1,0,2:T(8,128)} async-done(((f32[8,8,128,128]{3,1,0,2:T(8,128)}), f32[8,8,128,128]{3,1,0,2:T(8,128)}, u32[]{:S(2)}, u32[]{:S(2)}) %all-to-all-start.2) | async-done | bytes 4194336 | tf_op jit(solution)/shard_map/all_to_all | solution.py:62
  237.5 5.1 %all-to-all-start.1 = ((f32[8,128,8,128]{3,2,0,1:T(8,128)}), f32[8,128,8,128]{3,2,0,1:T(8,128)}, u32[]{:S(2)}, u32[]{:S(2)}) async-start(f32[8,128,8,128]{3,2,0,1:T(8,128)} %copy.15), calls=%async_computation.1 | async-start | bytes 8388608 | tf_op jit(solution)/shard_map/all_to_all | solution.py:65
  242.6 4.6 copy.22
  247.2 3.6 fusion.12
  250.8 3.4 fusion.17
  254.2 5.4 %copy.24 = f32[8,128,8,128]{3,2,0,1:T(8,128)} copy(f32[8,128,8,128]{1,3,2,0:T(8,128)} %fusion.17) | data formatting | bytes 8388608 | tf_op jit(solution)/shard_map/pzyx,zk->pkyx/transpose | solution.py:24
  259.6 75.3 %all-to-all-done.1 = f32[8,128,8,128]{3,2,0,1:T(8,128)} async-done(((f32[8,128,8,128]{3,2,0,1:T(8,128)}), f32[8,128,8,128]{3,2,0,1:T(8,128)}, u32[]{:S(2)}, u32[]{:S(2)}) %all-to-all-start.1) | async-done | bytes 4194336 | tf_op jit(solution)/shard_map/all_to_all | solution.py:65
  334.9 5.1 %all-to-all-start.3 = ((f32[8,128,8,128]{3,2,0,1:T(8,128)}), f32[8,128,8,128]{3,2,0,1:T(8,128)}, u32[]{:S(2)}, u32[]{:S(2)}) async-start(f32[8,128,8,128]{3,2,0,1:T(8,128)} %copy.24), calls=%async_computation.3 | async-start | bytes 8388608 | tf_op jit(solution)/shard_map/all_to_all | solution.py:65
  339.9 5.4 %fusion.8 = f32[8,8,128,128]{3,2,1,0:T(8,128)S(1)} fusion(f32[128,128,1,1]{1,0,3,2:T(8,128)S(1)} %copy-done.2, f32[8,8,16,8,128]{4,3,0,1,2:T(8,128)} %bitcast.11), kind=kOutput, calls=%fused_computation.9 | convolution fusion | flops 805306368 | bytes 8454144 | tf_op jit(solution)/shard_map/pzyx,yk->pzkx/dot_general | solution.py:24
  345.3 5.0 %fusion.6 = f32[8,8,128,128]{3,2,1,0:T(8,128)} fusion(f32[128,128,1,1]{1,0,3,2:T(8,128)S(1)} %copy-done.2, f32[8,8,128,128]{3,2,1,0:T(8,128)S(1)} %fusion.8), kind=kOutput, calls=%fused_computation.7 | convolution fusion | flops 805306368 | bytes 8454144 | tf_op jit(solution)/shard_map/pzyx,xk->pzyk/dot_general | solution.py:24
  350.4 81.9 %all-to-all-done.3 = f32[8,128,8,128]{3,2,0,1:T(8,128)} async-done(((f32[8,128,8,128]{3,2,0,1:T(8,128)}), f32[8,128,8,128]{3,2,0,1:T(8,128)}, u32[]{:S(2)}, u32[]{:S(2)}) %all-to-all-start.3) | async-done | bytes 4194336 | tf_op jit(solution)/shard_map/all_to_all | solution.py:65
  432.3 5.6 %fusion.2 = f32[8,8,128,128]{3,2,1,0:T(8,128)S(1)} fusion(f32[128,128,1,1]{1,0,3,2:T(8,128)S(1)} %copy-done.2, f32[8,8,16,8,128]{4,3,0,1,2:T(8,128)} %bitcast.24), kind=kOutput, calls=%fused_computation.2 | convolution fusion | flops 805306368 | bytes 8454144 | tf_op jit(solution)/shard_map/pzyx,yk->pzkx/dot_general | solution.py:24
  437.9 4.1 multiply_reduce_fusion.2
  442.5 1.5 multiply_reduce_fusion
  444.0 1.6 add.74
  445.6 21.8 %collective-permute-done.1 = f32[2,8,128,128]{3,2,1,0:T(8,128)S(1)} collective-permute-done((f32[2,8,128,128]{3,2,1,0:T(8,128)S(1)}, f32[2,8,128,128]{3,2,1,0:T(8,128)S(1)}, u32[]{:S(2)}, u32[]{:S(2)}) %collective-permute-start.1) | collective-permute-done | bytes 1048608 | tf_op jit(solution)/shard_map/ppermute | solution.py:44
  467.4 1.1 add.73
  (16 shorter events, 1.4 us)
Async XLA Ops:
  0.6 30.2 %copy-start.2 = (f32[128,128,1,1]{1,0,3,2:T(8,128)S(1)}, f32[128,128,1,1]{1,0,3,2:T(8,128)}, u32[]{:S(2)}) copy-start(f32[128,128,1,1]{1,0,3,2:T(8,128)} %constant.29) | copy-start | bytes 196612
  0.6 25.2 %collective-permute-start = (f32[2,8,128,128]{3,2,1,0:T(8,128)}, f32[2,8,128,128]{3,2,1,0:T(8,128)S(1)}, u32[]{:S(2)}, u32[]{:S(2)}) collective-permute-start(f32[2,8,128,128]{3,2,1,0:T(8,128)} %param.3), channel_id=1, source_target_pairs={{16,0},{0,16},{17,1},{1,17},{18,2},{2,18},{19,3},{3,19},{20,4},{4,... | collective-permute-start | bytes 3145736 | tf_op jit(solution)/shard_map/ppermute | solution.py:44
  41.6 98.6 %all-to-all-start = ((f32[8,8,128,128]{3,1,0,2:T(8,128)}), f32[8,8,128,128]{3,1,0,2:T(8,128)}, u32[]{:S(2)}, u32[]{:S(2)}) async-start(f32[8,8,128,128]{3,1,0,2:T(8,128)} %copy.12), calls=%async_computation | async-start | bytes 8388608 | tf_op jit(solution)/shard_map/all_to_all | solution.py:62
  140.1 97.4 %all-to-all-start.2 = ((f32[8,8,128,128]{3,1,0,2:T(8,128)}), f32[8,8,128,128]{3,1,0,2:T(8,128)}, u32[]{:S(2)}, u32[]{:S(2)}) async-start(f32[8,8,128,128]{3,1,0,2:T(8,128)} %copy.21), calls=%async_computation.2 | async-start | bytes 8388608 | tf_op jit(solution)/shard_map/all_to_all | solution.py:62
  145.5 4.7 copy-start.4
  237.5 97.4 %all-to-all-start.1 = ((f32[8,128,8,128]{3,2,0,1:T(8,128)}), f32[8,128,8,128]{3,2,0,1:T(8,128)}, u32[]{:S(2)}, u32[]{:S(2)}) async-start(f32[8,128,8,128]{3,2,0,1:T(8,128)} %copy.15), calls=%async_computation.1 | async-start | bytes 8388608 | tf_op jit(solution)/shard_map/all_to_all | solution.py:65
  334.9 97.4 %all-to-all-start.3 = ((f32[8,128,8,128]{3,2,0,1:T(8,128)}), f32[8,128,8,128]{3,2,0,1:T(8,128)}, u32[]{:S(2)}, u32[]{:S(2)}) async-start(f32[8,128,8,128]{3,2,0,1:T(8,128)} %copy.24), calls=%async_computation.3 | async-start | bytes 8388608 | tf_op jit(solution)/shard_map/all_to_all | solution.py:65
  432.3 5.6 %copy-start = (f32[8,8,128,128]{3,2,1,0:T(8,128)S(1)}, f32[8,8,128,128]{3,2,1,0:T(8,128)}, u32[]{:S(2)}) copy-start(f32[8,8,128,128]{3,2,1,0:T(8,128)} %fusion.6) | copy-start | bytes 12582916
  432.3 5.6 %copy-start.1 = (f32[4,8,128,128]{3,2,1,0:T(8,128)S(1)}, f32[4,8,128,128]{3,2,1,0:T(8,128)}, u32[]{:S(2)}) copy-start(f32[4,8,128,128]{3,2,1,0:T(8,128)} %param.4) | copy-start | bytes 6291460
  437.9 4.7 copy-start.3
  442.0 25.4 %collective-permute-start.1 = (f32[2,8,128,128]{3,2,1,0:T(8,128)S(1)}, f32[2,8,128,128]{3,2,1,0:T(8,128)S(1)}, u32[]{:S(2)}, u32[]{:S(2)}) collective-permute-start(f32[2,8,128,128]{3,2,1,0:T(8,128)S(1)} %get-tuple-element.2), channel_id=1, source_target_pairs={{16,0},{0,16},{17,1},{1,17},{18,2},{2,18},{19,3},{3,19},{20,4},{4,... | collective-permute-start | bytes 3145736 | tf_op jit(solution)/shard_map/ppermute | solution.py:44
where the time goes:
time: 469 us; the launch traced here: 468 us
  waiting for transfers between devices  358 us (76%)
  matrix products  46.6 us (10%)
  local copies, waits for them, and re-layouts  30.9 us (7%)
  starting transfers between devices  22.6 us (5%)
  other arithmetic  9.47 us (2%)
    all_to_all x2, waiting for transfers between devices, pencils(): lax.all_to_all(field, 'slab', split_axis=1, concat_axis=2, tiled=True)  157 us
    all_to_all x2, waiting for transfers between devices, pencils(): lax.all_to_all(field, 'slab', split_axis=2, concat_axis=1, tiled=True)  155 us
    dot_general x12, matrix products, apply_table(): return jnp.einsum(pattern, field, table, precision=precision)  46.6 us
    ppermute x2, waiting for transfers between devices, band_shift(): return lax.ppermute(block, 'band', route)  46.4 us
    transpose x4, local copies, waits for them, and re-layouts, apply_table(): return jnp.einsum(pattern, field, table, precision=precision)  21.6 us
    all_to_all x2, starting transfers between devices, pencils(): lax.all_to_all(field, 'slab', split_axis=2, concat_axis=1, tiled=True)  11.3 us
    all_to_all x2, starting transfers between devices, pencils(): lax.all_to_all(field, 'slab', split_axis=1, concat_axis=2, tiled=True)  10.1 us
  transfers between devices with their start and end apart: 6, of which 6 were waited for; matrix products, arithmetic and copies ran while one was open for 13% of the time, Pallas kernels for 0%

commit v1 on v0

--- a/solution.py
+++ b/solution.py
@@ -9,6 +9,29 @@
 STEPS = 2
 coulomb_scale = 46.9 * 46.9 / math.pi
 precision = lax.Precision.HIGH
+
+
+def in_blocks(x, dim, length):
+    dims = x.shape
+    parts = x.reshape(*dims[:dim], length, dims[dim] // length, *dims[dim + 1 :])
+    return jnp.moveaxis(parts, dim, 0)
+
+
+def laid_out(blocks, dim):
+    blocks = jnp.moveaxis(blocks, 0, dim)
+    lengths = blocks.shape
+    return blocks.reshape(*lengths[:dim], lengths[dim] * lengths[dim + 1], *lengths[dim + 2 :])
+
+
+def rotated_exchange(shard, axis, split_dim, concat_dim):
+    count, mine = (lax.axis_size(axis), lax.axis_index(axis))
+    blocks = in_blocks(shard, split_dim, count)
+    outs = [blocks[mine]]
+    for hop in range(1, count):
+        sent = blocks[(mine + hop) % count]
+        outs.append(lax.ppermute(sent, axis, [(i, (i + hop) % count) for i in range(count)]))
+    blocks = jnp.stack(outs)[(mine - jnp.arange(count)) % count]
+    return laid_out(blocks, concat_dim)
 
 
 def cas_table(length):
@@ -62,7 +85,7 @@
         field = lax.all_to_all(field, "slab", split_axis=2, concat_axis=1, tiled=True)
         field = apply_table("pzyx,zk->pkyx", field, table) * kernel
         field = apply_table("pzyx,zk->pkyx", field, table)
-        field = lax.all_to_all(field, "slab", split_axis=1, concat_axis=2, tiled=True)
+        field = rotated_exchange(field, "slab", 1, 2)
         field = apply_table("pzyx,yk->pzkx", field, table)
         field = apply_table("pzyx,xk->pzyk", field, table)
         potential = field.reshape((own_count, part_count) + own.shape[1:])

time: 469 us -> 537 us (1.14)
  the two profiles are of different devices: /device:TPU:14 before, /device:TPU:27 now
where the time goes in v1:
time: 537 us; the launch traced here: 530 us
  waiting for transfers between devices  304 us (57%)
  starting transfers between devices  104 us (19%)
  local copies, waits for them, and re-layouts  66.3 us (12%)
  matrix products  44.9 us (8%)
  other arithmetic  9.53 us (2%)
    all_to_all x2, waiting for transfers between devices, pencils(): lax.all_to_all(field, 'slab', split_axis=2, concat_axis=1, tiled=True)  160 us
    ppermute x30, waiting for transfers between devices, rotated_exchange(): lax.ppermute(sent, axis, [(i, (i + hop) % count) for i in range(count)])  101 us
    ppermute x30, starting transfers between devices, rotated_exchange(): lax.ppermute(sent, axis, [(i, (i + hop) % count) for i in range(count)])  87.3 us
    dot_general x12, matrix products, apply_table(): return jnp.einsum(pattern, field, table, precision=precision)  44.9 us
    ppermute x2, waiting for transfers between devices, band_shift(): return lax.ppermute(block, 'band', route)  43.1 us
    unnamed x50, local copies, waits for them, and re-layouts  26.4 us
    all_to_all x2, starting transfers between devices, pencils(): lax.all_to_all(field, 'slab', split_axis=2, concat_axis=1, tiled=True)  13.7 us
    transpose x2, local copies, waits for them, and re-layouts, apply_table(): return jnp.einsum(pattern, field, table, precision=precision)  10.8 us
  transfers between devices with their start and end apart: 34, of which 20 were waited for; matrix products, arithmetic and copies ran while one was open for 14% of the time, Pallas kernels for 0%

profile of v1, /device:TPU:27, one launch (start us, length us, event | category | flops | bytes accessed | tf_op | source)
XLA Modules:
  0.0 530.1 jit_solution(11341566041902980664)
XLA Ops:
  1.9 23.0 %collective-permute-done.15 = f32[2,8,128,128]{3,2,1,0:T(8,128)S(1)} collective-permute-done((f32[2,8,128,128]{3,2,1,0:T(8,128)}, f32[2,8,128,128]{3,2,1,0:T(8,128)S(1)}, u32[]{:S(2)}, u32[]{:S(2)}) %collective-permute-start.15) | collective-permute-done | bytes 1048608 | tf_op jit(solution)/shard_map/ppermute | solution.py:67
  24.9 5.1 broadcast_multiply_fusion.1
  35.3 5.4 %copy.85 = f32[8,8,128,128]{3,1,0,2:T(8,128)} copy(f32[8,8,128,128]{2,3,1,0:T(8,128)} %convolution_bitcast_fusion) | data formatting | bytes 8388608 | tf_op jit(solution)/shard_map/pzyx,yk->pzkx/transpose | solution.py:47
  40.7 7.2 %all-to-all-start.1 = ((f32[8,8,128,128]{3,1,0,2:T(8,128)}), f32[8,8,128,128]{3,1,0,2:T(8,128)}, u32[]{:S(2)}, u32[]{:S(2)}) async-start(f32[8,8,128,128]{3,1,0,2:T(8,128)} %copy.85), calls=%async_computation.1 | async-start | bytes 8388608 | tf_op jit(solution)/shard_map/all_to_all | solution.py:85
  47.9 4.1 fusion.28
  55.3 5.4 %copy.60 = f32[8,8,128,128]{3,1,0,2:T(8,128)} copy(f32[8,8,128,128]{2,3,1,0:T(8,128)} %convolution_bitcast_fusion.1) | data formatting | bytes 8388608 | tf_op jit(solution)/shard_map/pzyx,yk->pzkx/transpose | solution.py:47
  60.7 78.8 %all-to-all-done.1 = f32[8,8,128,128]{3,1,0,2:T(8,128)} async-done(((f32[8,8,128,128]{3,1,0,2:T(8,128)}), f32[8,8,128,128]{3,1,0,2:T(8,128)}, u32[]{:S(2)}, u32[]{:S(2)}) %all-to-all-start.1) | async-done | bytes 4194336 | tf_op jit(solution)/shard_map/all_to_all | solution.py:85
  139.4 6.5 %all-to-all-start = ((f32[8,8,128,128]{3,1,0,2:T(8,128)}), f32[8,8,128,128]{3,1,0,2:T(8,128)}, u32[]{:S(2)}, u32[]{:S(2)}) async-start(f32[8,8,128,128]{3,1,0,2:T(8,128)} %copy.60), calls=%async_computation | async-start | bytes 8388608 | tf_op jit(solution)/shard_map/all_to_all | solution.py:85
  146.5 4.7 copy.86
  151.2 5.0 fusion.11
  156.1 81.1 %all-to-all-done = f32[8,8,128,128]{3,1,0,2:T(8,128)} async-done(((f32[8,8,128,128]{3,1,0,2:T(8,128)}), f32[8,8,128,128]{3,1,0,2:T(8,128)}, u32[]{:S(2)}, u32[]{:S(2)}) %all-to-all-start) | async-done | bytes 4194336 | tf_op jit(solution)/shard_map/all_to_all | solution.py:85
  237.3 4.6 copy.61
  266.1 6.6 %collective-permute-done = f32[8,8,8,128]{3,2,1,0:T(8,128)S(1)} collective-permute-done((f32[8,8,8,128]{3,2,1,0:T(8,128)S(1)}, f32[8,8,8,128]{3,2,1,0:T(8,128)S(1)}, u32[]{:S(2)}, u32[]{:S(2)}) %collective-permute-start) | collective-permute-done | bytes 262176 | tf_op jit(solution)/shard_map/ppermute | solution.py:32
  273.4 4.9 collective-permute-done.1
  287.2 4.4 collective-permute-start.5
  292.8 13.8 %collective-permute-start.6 = (f32[8,8,8,128]{3,2,1,0:T(8,128)S(1)}, f32[8,8,8,128]{3,2,1,0:T(8,128)S(1)}, u32[]{:S(2)}, u32[]{:S(2)}) collective-permute-start(f32[8,8,8,128]{3,2,1,0:T(8,128)S(1)} %bitcast.257), channel_id=1, source_target_pairs={{0,7},{1,8},{2,9},{3,10},{4,11},{5,12},{6,13},{7,14},{8,15},{9,0},... | collective-permute-start | bytes 786440 | tf_op jit(solution)/shard_map/ppermute | solution.py:32
  307.3 12.9 %collective-permute-start.7 = (f32[8,8,8,128]{3,2,1,0:T(8,128)S(1)}, f32[8,8,8,128]{3,2,1,0:T(8,128)S(1)}, u32[]{:S(2)}, u32[]{:S(2)}) collective-permute-start(f32[8,8,8,128]{3,2,1,0:T(8,128)S(1)} %bitcast.256), channel_id=1, source_target_pairs={{0,8},{1,9},{2,10},{3,11},{4,12},{5,13},{6,14},{7,15},{8,0},{9,1},... | collective-permute-start | bytes 786440 | tf_op jit(solution)/shard_map/ppermute | solution.py:32
  321.7 18.7 %collective-permute-done.7 = f32[8,8,8,128]{3,2,1,0:T(8,128)S(1)} collective-permute-done((f32[8,8,8,128]{3,2,1,0:T(8,128)S(1)}, f32[8,8,8,128]{3,2,1,0:T(8,128)S(1)}, u32[]{:S(2)}, u32[]{:S(2)}) %collective-permute-start.7) | collective-permute-done | bytes 262176 | tf_op jit(solution)/shard_map/ppermute | solution.py:32
  341.8 28.9 %collective-permute-done.9 = f32[8,8,8,128]{3,2,1,0:T(8,128)S(1)} collective-permute-done((f32[8,8,8,128]{3,2,1,0:T(8,128)S(1)}, f32[8,8,8,128]{3,2,1,0:T(8,128)S(1)}, u32[]{:S(2)}, u32[]{:S(2)}) %collective-permute-start.9) | collective-permute-done | bytes 262176 | tf_op jit(solution)/shard_map/ppermute | solution.py:32
  372.7 5.8 %collective-permute-done.11 = f32[8,8,8,128]{3,2,1,0:T(8,128)S(1)} collective-permute-done((f32[8,8,8,128]{3,2,1,0:T(8,128)S(1)}, f32[8,8,8,128]{3,2,1,0:T(8,128)S(1)}, u32[]{:S(2)}, u32[]{:S(2)}) %collective-permute-start.11) | collective-permute-done | bytes 262176 | tf_op jit(solution)/shard_map/ppermute | solution.py:32
  381.6 5.0 collective-permute-done.13
  391.5 5.0 gather_fusion
  396.5 5.4 %fusion.7 = f32[8,8,128,128]{3,2,1,0:T(8,128)S(1)} fusion(f32[128,128,1,1]{1,0,3,2:T(8,128)S(1)} %copy-done.3, f32[16,8,8,8,128]{4,3,2,1,0:T(8,128)} %gather_fusion), kind=kOutput, calls=%fused_computation.10 | convolution fusion | flops 805306368 | bytes 8454144 | tf_op jit(solution)/shard_map/pzyx,yk->pzkx/dot_general | solution.py:47
  401.9 5.1 fusion.5
  421.3 17.3 %collective-permute-start.26 = (f32[8,8,8,128]{3,2,1,0:T(8,128)S(1)}, f32[8,8,8,128]{3,2,1,0:T(8,128)S(1)}, u32[]{:S(2)}, u32[]{:S(2)}) collective-permute-start(f32[8,8,8,128]{3,2,1,0:T(8,128)S(1)} %bitcast.242), channel_id=1, source_target_pairs={{0,11},{1,12},{2,13},{3,14},{4,15},{5,0},{6,1},{7,2},{8,3},{9,4},{... | collective-permute-start | bytes 786440 | tf_op jit(solution)/shard_map/ppermute | solution.py:32
  439.3 9.4 %collective-permute-start.27 = (f32[8,8,8,128]{3,2,1,0:T(8,128)S(1)}, f32[8,8,8,128]{3,2,1,0:T(8,128)S(1)}, u32[]{:S(2)}, u32[]{:S(2)}) collective-permute-start(f32[8,8,8,128]{3,2,1,0:T(8,128)S(1)} %bitcast.241), channel_id=1, source_target_pairs={{0,12},{1,13},{2,14},{3,15},{4,0},{5,1},{6,2},{7,3},{8,4},{9,5},{1... | collective-permute-start | bytes 786440 | tf_op jit(solution)/shard_map/ppermute | solution.py:32
  449.4 15.4 %collective-permute-done.23 = f32[8,8,8,128]{3,2,1,0:T(8,128)S(1)} collective-permute-done((f32[8,8,8,128]{3,2,1,0:T(8,128)S(1)}, f32[8,8,8,128]{3,2,1,0:T(8,128)S(1)}, u32[]{:S(2)}, u32[]{:S(2)}) %collective-permute-start.23) | collective-permute-done | bytes 262176 | tf_op jit(solution)/shard_map/ppermute | solution.py:32
  470.0 14.1 %collective-permute-start.30 = (f32[8,8,8,128]{3,2,1,0:T(8,128)S(1)}, f32[8,8,8,128]{3,2,1,0:T(8,128)S(1)}, u32[]{:S(2)}, u32[]{:S(2)}) collective-permute-start(f32[8,8,8,128]{3,2,1,0:T(8,128)S(1)} %bitcast.238), channel_id=1, source_target_pairs={{0,15},{1,0},{2,1},{3,2},{4,3},{5,4},{6,5},{7,6},{8,7},{9,8},{10,9... | collective-permute-start | bytes 786440 | tf_op jit(solution)/shard_map/ppermute | solution.py:32
  489.6 5.0 gather_fusion.1
  494.6 5.5 %fusion.2 = f32[8,8,128,128]{3,2,1,0:T(8,128)S(1)} fusion(f32[128,128,1,1]{1,0,3,2:T(8,128)S(1)} %copy-done.3, f32[16,8,8,8,128]{4,3,2,1,0:T(8,128)} %gather_fusion.1), kind=kOutput, calls=%fused_computation.4 | convolution fusion | flops 805306368 | bytes 8454144 | tf_op jit(solution)/shard_map/pzyx,yk->pzkx/dot_general | solution.py:47
  500.2 4.1 multiply_reduce_fusion.2
  508.7 20.2 %collective-permute-done.31 = f32[2,8,128,128]{3,2,1,0:T(8,128)S(1)} collective-permute-done((f32[2,8,128,128]{3,2,1,0:T(8,128)S(1)}, f32[2,8,128,128]{3,2,1,0:T(8,128)S(1)}, u32[]{:S(2)}, u32[]{:S(2)}) %collective-permute-start.31) | collective-permute-done | bytes 1048608 | tf_op jit(solution)/shard_map/ppermute | solution.py:67
  (148 shorter events, 90.4 us)
Async XLA Ops:
  0.6 24.3 %collective-permute-start.15 = (f32[2,8,128,128]{3,2,1,0:T(8,128)}, f32[2,8,128,128]{3,2,1,0:T(8,128)S(1)}, u32[]{:S(2)}, u32[]{:S(2)}) collective-permute-start(f32[2,8,128,128]{3,2,1,0:T(8,128)} %param.3), channel_id=1, source_target_pairs={{16,0},{0,16},{17,1},{1,17},{18,2},{2,18},{19,3},{3,19},{20,4},{4,... | collective-permute-start | bytes 3145736 | tf_op jit(solution)/shard_map/ppermute | solution.py:67
  40.7 98.7 %all-to-all-start.1 = ((f32[8,8,128,128]{3,1,0,2:T(8,128)}), f32[8,8,128,128]{3,1,0,2:T(8,128)}, u32[]{:S(2)}, u32[]{:S(2)}) async-start(f32[8,8,128,128]{3,1,0,2:T(8,128)} %copy.85), calls=%async_computation.1 | async-start | bytes 8388608 | tf_op jit(solution)/shard_map/all_to_all | solution.py:85
  139.4 97.8 %all-to-all-start = ((f32[8,8,128,128]{3,1,0,2:T(8,128)}), f32[8,8,128,128]{3,1,0,2:T(8,128)}, u32[]{:S(2)}, u32[]{:S(2)}) async-start(f32[8,8,128,128]{3,1,0,2:T(8,128)} %copy.60), calls=%async_computation | async-start | bytes 8388608 | tf_op jit(solution)/shard_map/all_to_all | solution.py:85
  252.1 154.9 %collective-permute-start.16 = (f32[8,8,8,128]{3,2,1,0:T(8,128)}, f32[8,8,8,128]{3,2,1,0:T(8,128)}, u32[]{:S(2)}, u32[]{:S(2)}) collective-permute-start(f32[8,8,8,128]{3,2,1,0:T(8,128)} %bitcast.216), channel_id=1, source_target_pairs={{0,1},{1,2},{2,3},{3,4},{4,5},{5,6},{6,7},{7,8},{8,9},{9,10},{10,1... | collective-permute-start | bytes 786440 | tf_op jit(solution)/shard_map/ppermute | solution.py:32
  252.1 156.6 %collective-permute-start.17 = (f32[8,8,8,128]{3,2,1,0:T(8,128)}, f32[8,8,8,128]{3,2,1,0:T(8,128)}, u32[]{:S(2)}, u32[]{:S(2)}) collective-permute-start(f32[8,8,8,128]{3,2,1,0:T(8,128)} %bitcast.215), channel_id=1, source_target_pairs={{0,2},{1,3},{2,4},{3,5},{4,6},{5,7},{6,8},{7,9},{8,10},{9,11},{10,... | collective-permute-start | bytes 786440 | tf_op jit(solution)/shard_map/ppermute | solution.py:32
  252.1 159.6 %collective-permute-start.18 = (f32[8,8,8,128]{3,2,1,0:T(8,128)S(1)}, f32[8,8,8,128]{3,2,1,0:T(8,128)}, u32[]{:S(2)}, u32[]{:S(2)}) collective-permute-start(f32[8,8,8,128]{3,2,1,0:T(8,128)S(1)} %bitcast.244), channel_id=1, source_target_pairs={{0,3},{1,4},{2,5},{3,6},{4,7},{5,8},{6,9},{7,10},{8,11},{9,12},{10... | collective-permute-start | bytes 786440 | tf_op jit(solution)/shard_map/ppermute | solution.py:32
  253.4 19.3 %collective-permute-start = (f32[8,8,8,128]{3,2,1,0:T(8,128)S(1)}, f32[8,8,8,128]{3,2,1,0:T(8,128)S(1)}, u32[]{:S(2)}, u32[]{:S(2)}) collective-permute-start(f32[8,8,8,128]{3,2,1,0:T(8,128)S(1)} %bitcast.260), channel_id=1, source_target_pairs={{0,1},{1,2},{2,3},{3,4},{4,5},{5,6},{6,7},{7,8},{8,9},{9,10},{10,1... | collective-permute-start | bytes 786440 | tf_op jit(solution)/shard_map/ppermute | solution.py:32
  257.3 21.0 %collective-permute-start.1 = (f32[8,8,8,128]{3,2,1,0:T(8,128)S(1)}, f32[8,8,8,128]{3,2,1,0:T(8,128)S(1)}, u32[]{:S(2)}, u32[]{:S(2)}) collective-permute-start(f32[8,8,8,128]{3,2,1,0:T(8,128)S(1)} %bitcast.258), channel_id=1, source_target_pairs={{0,2},{1,3},{2,4},{3,5},{4,6},{5,7},{6,8},{7,9},{8,10},{9,11},{10,... | collective-permute-start | bytes 786440 | tf_op jit(solution)/shard_map/ppermute | solution.py:32
  272.7 11.0 %collective-permute-start.2 = (f32[8,8,8,128]{3,2,1,0:T(8,128)S(1)}, f32[8,8,8,128]{3,2,1,0:T(8,128)S(1)}, u32[]{:S(2)}, u32[]{:S(2)}) collective-permute-start(f32[8,8,8,128]{3,2,1,0:T(8,128)S(1)} %bitcast.263), channel_id=1, source_target_pairs={{0,3},{1,4},{2,5},{3,6},{4,7},{5,8},{6,9},{7,10},{8,11},{9,12},{10... | collective-permute-start | bytes 786440 | tf_op jit(solution)/shard_map/ppermute | solution.py:32
  278.3 8.8 %collective-permute-start.3 = (f32[8,8,8,128]{3,2,1,0:T(8,128)S(1)}, f32[8,8,8,128]{3,2,1,0:T(8,128)S(1)}, u32[]{:S(2)}, u32[]{:S(2)}) collective-permute-start(f32[8,8,8,128]{3,2,1,0:T(8,128)S(1)} %bitcast.262), channel_id=1, source_target_pairs={{0,4},{1,5},{2,6},{3,7},{4,8},{5,9},{6,10},{7,11},{8,12},{9,13},{1... | collective-permute-start | bytes 786440 | tf_op jit(solution)/shard_map/ppermute | solution.py:32
  283.7 9.1 %collective-permute-start.4 = (f32[8,8,8,128]{3,2,1,0:T(8,128)S(1)}, f32[8,8,8,128]{3,2,1,0:T(8,128)S(1)}, u32[]{:S(2)}, u32[]{:S(2)}) collective-permute-start(f32[8,8,8,128]{3,2,1,0:T(8,128)S(1)} %bitcast.261), channel_id=1, source_target_pairs={{0,5},{1,6},{2,7},{3,8},{4,9},{5,10},{6,11},{7,12},{8,13},{9,14},{... | collective-permute-start | bytes 786440 | tf_op jit(solution)/shard_map/ppermute | solution.py:32
  287.2 20.1 %collective-permute-start.5 = (f32[8,8,8,128]{3,2,1,0:T(8,128)S(1)}, f32[8,8,8,128]{3,2,1,0:T(8,128)S(1)}, u32[]{:S(2)}, u32[]{:S(2)}) collective-permute-start(f32[8,8,8,128]{3,2,1,0:T(8,128)S(1)} %bitcast.259), channel_id=1, source_target_pairs={{0,6},{1,7},{2,8},{3,9},{4,10},{5,11},{6,12},{7,13},{8,14},{9,15},... | collective-permute-start | bytes 786440 | tf_op jit(solution)/shard_map/ppermute | solution.py:32
  292.8 28.1 %collective-permute-start.6 = (f32[8,8,8,128]{3,2,1,0:T(8,128)S(1)}, f32[8,8,8,128]{3,2,1,0:T(8,128)S(1)}, u32[]{:S(2)}, u32[]{:S(2)}) collective-permute-start(f32[8,8,8,128]{3,2,1,0:T(8,128)S(1)} %bitcast.257), channel_id=1, source_target_pairs={{0,7},{1,8},{2,9},{3,10},{4,11},{5,12},{6,13},{7,14},{8,15},{9,0},... | collective-permute-start | bytes 786440 | tf_op jit(solution)/shard_map/ppermute | solution.py:32
  307.3 33.0 %collective-permute-start.7 = (f32[8,8,8,128]{3,2,1,0:T(8,128)S(1)}, f32[8,8,8,128]{3,2,1,0:T(8,128)S(1)}, u32[]{:S(2)}, u32[]{:S(2)}) collective-permute-start(f32[8,8,8,128]{3,2,1,0:T(8,128)S(1)} %bitcast.256), channel_id=1, source_target_pairs={{0,8},{1,9},{2,10},{3,11},{4,12},{5,13},{6,14},{7,15},{8,0},{9,1},... | collective-permute-start | bytes 786440 | tf_op jit(solution)/shard_map/ppermute | solution.py:32
  320.9 20.1 %collective-permute-start.8 = (f32[8,8,8,128]{3,2,1,0:T(8,128)S(1)}, f32[8,8,8,128]{3,2,1,0:T(8,128)S(1)}, u32[]{:S(2)}, u32[]{:S(2)}) collective-permute-start(f32[8,8,8,128]{3,2,1,0:T(8,128)S(1)} %bitcast.255), channel_id=1, source_target_pairs={{0,9},{1,10},{2,11},{3,12},{4,13},{5,14},{6,15},{7,0},{8,1},{9,2},... | collective-permute-start | bytes 786440 | tf_op jit(solution)/shard_map/ppermute | solution.py:32
  340.3 30.4 %collective-permute-start.9 = (f32[8,8,8,128]{3,2,1,0:T(8,128)S(1)}, f32[8,8,8,128]{3,2,1,0:T(8,128)S(1)}, u32[]{:S(2)}, u32[]{:S(2)}) collective-permute-start(f32[8,8,8,128]{3,2,1,0:T(8,128)S(1)} %bitcast.254), channel_id=1, source_target_pairs={{0,10},{1,11},{2,12},{3,13},{4,14},{5,15},{6,0},{7,1},{8,2},{9,3},... | collective-permute-start | bytes 786440 | tf_op jit(solution)/shard_map/ppermute | solution.py:32
  341.1 31.0 %collective-permute-start.10 = (f32[8,8,8,128]{3,2,1,0:T(8,128)S(1)}, f32[8,8,8,128]{3,2,1,0:T(8,128)S(1)}, u32[]{:S(2)}, u32[]{:S(2)}) collective-permute-start(f32[8,8,8,128]{3,2,1,0:T(8,128)S(1)} %bitcast.253), channel_id=1, source_target_pairs={{0,11},{1,12},{2,13},{3,14},{4,15},{5,0},{6,1},{7,2},{8,3},{9,4},{... | collective-permute-start | bytes 786440 | tf_op jit(solution)/shard_map/ppermute | solution.py:32
  372.0 8.8 %collective-permute-start.12 = (f32[8,8,8,128]{3,2,1,0:T(8,128)S(1)}, f32[8,8,8,128]{3,2,1,0:T(8,128)S(1)}, u32[]{:S(2)}, u32[]{:S(2)}) collective-permute-start(f32[8,8,8,128]{3,2,1,0:T(8,128)S(1)} %bitcast.251), channel_id=1, source_target_pairs={{0,13},{1,14},{2,15},{3,0},{4,1},{5,2},{6,3},{7,4},{8,5},{9,6},{10... | collective-permute-start | bytes 786440 | tf_op jit(solution)/shard_map/ppermute | solution.py:32
  380.8 10.0 %collective-permute-start.14 = (f32[8,8,8,128]{3,2,1,0:T(8,128)S(1)}, f32[8,8,8,128]{3,2,1,0:T(8,128)S(1)}, u32[]{:S(2)}, u32[]{:S(2)}) collective-permute-start(f32[8,8,8,128]{3,2,1,0:T(8,128)S(1)} %bitcast.249), channel_id=1, source_target_pairs={{0,15},{1,0},{2,1},{3,2},{4,3},{5,4},{6,5},{7,6},{8,7},{9,8},{10,9... | collective-permute-start | bytes 786440 | tf_op jit(solution)/shard_map/ppermute | solution.py:32
  386.5 27.4 %collective-permute-start.19 = (f32[8,8,8,128]{3,2,1,0:T(8,128)}, f32[8,8,8,128]{3,2,1,0:T(8,128)}, u32[]{:S(2)}, u32[]{:S(2)}) collective-permute-start(f32[8,8,8,128]{3,2,1,0:T(8,128)} %bitcast.213), channel_id=1, source_target_pairs={{0,4},{1,5},{2,6},{3,7},{4,8},{5,9},{6,10},{7,11},{8,12},{9,13},{1... | collective-permute-start | bytes 786440 | tf_op jit(solution)/shard_map/ppermute | solution.py:32
  390.8 26.6 %collective-permute-start.20 = (f32[8,8,8,128]{3,2,1,0:T(8,128)}, f32[8,8,8,128]{3,2,1,0:T(8,128)}, u32[]{:S(2)}, u32[]{:S(2)}) collective-permute-start(f32[8,8,8,128]{3,2,1,0:T(8,128)} %bitcast.212), channel_id=1, source_target_pairs={{0,5},{1,6},{2,7},{3,8},{4,9},{5,10},{6,11},{7,12},{8,13},{9,14},{... | collective-permute-start | bytes 786440 | tf_op jit(solution)/shard_map/ppermute | solution.py:32
  407.0 14.3 %collective-permute-start.21 = (f32[8,8,8,128]{3,2,1,0:T(8,128)S(1)}, f32[8,8,8,128]{3,2,1,0:T(8,128)S(1)}, u32[]{:S(2)}, u32[]{:S(2)}) collective-permute-start(f32[8,8,8,128]{3,2,1,0:T(8,128)S(1)} %bitcast.248), channel_id=1, source_target_pairs={{0,6},{1,7},{2,8},{3,9},{4,10},{5,11},{6,12},{7,13},{8,14},{9,15},... | collective-permute-start | bytes 786440 | tf_op jit(solution)/shard_map/ppermute | solution.py:32
  408.7 30.6 %collective-permute-start.22 = (f32[8,8,8,128]{3,2,1,0:T(8,128)S(1)}, f32[8,8,8,128]{3,2,1,0:T(8,128)S(1)}, u32[]{:S(2)}, u32[]{:S(2)}) collective-permute-start(f32[8,8,8,128]{3,2,1,0:T(8,128)S(1)} %bitcast.247), channel_id=1, source_target_pairs={{0,7},{1,8},{2,9},{3,10},{4,11},{5,12},{6,13},{7,14},{8,15},{9,0},... | collective-permute-start | bytes 786440 | tf_op jit(solution)/shard_map/ppermute | solution.py:32
  411.7 53.1 %collective-permute-start.23 = (f32[8,8,8,128]{3,2,1,0:T(8,128)S(1)}, f32[8,8,8,128]{3,2,1,0:T(8,128)S(1)}, u32[]{:S(2)}, u32[]{:S(2)}) collective-permute-start(f32[8,8,8,128]{3,2,1,0:T(8,128)S(1)} %bitcast.246), channel_id=1, source_target_pairs={{0,8},{1,9},{2,10},{3,11},{4,12},{5,13},{6,14},{7,15},{8,0},{9,1},... | collective-permute-start | bytes 786440 | tf_op jit(solution)/shard_map/ppermute | solution.py:32
  414.0 53.4 %collective-permute-start.24 = (f32[8,8,8,128]{3,2,1,0:T(8,128)S(1)}, f32[8,8,8,128]{3,2,1,0:T(8,128)S(1)}, u32[]{:S(2)}, u32[]{:S(2)}) collective-permute-start(f32[8,8,8,128]{3,2,1,0:T(8,128)S(1)} %bitcast.245), channel_id=1, source_target_pairs={{0,9},{1,10},{2,11},{3,12},{4,13},{5,14},{6,15},{7,0},{8,1},{9,2},... | collective-permute-start | bytes 786440 | tf_op jit(solution)/shard_map/ppermute | solution.py:32
  417.4 52.6 %collective-permute-start.25 = (f32[8,8,8,128]{3,2,1,0:T(8,128)S(1)}, f32[8,8,8,128]{3,2,1,0:T(8,128)S(1)}, u32[]{:S(2)}, u32[]{:S(2)}) collective-permute-start(f32[8,8,8,128]{3,2,1,0:T(8,128)S(1)} %bitcast.243), channel_id=1, source_target_pairs={{0,10},{1,11},{2,12},{3,13},{4,14},{5,15},{6,0},{7,1},{8,2},{9,3},... | collective-permute-start | bytes 786440 | tf_op jit(solution)/shard_map/ppermute | solution.py:32
  421.3 64.7 %collective-permute-start.26 = (f32[8,8,8,128]{3,2,1,0:T(8,128)S(1)}, f32[8,8,8,128]{3,2,1,0:T(8,128)S(1)}, u32[]{:S(2)}, u32[]{:S(2)}) collective-permute-start(f32[8,8,8,128]{3,2,1,0:T(8,128)S(1)} %bitcast.242), channel_id=1, source_target_pairs={{0,11},{1,12},{2,13},{3,14},{4,15},{5,0},{6,1},{7,2},{8,3},{9,4},{... | collective-permute-start | bytes 786440 | tf_op jit(solution)/shard_map/ppermute | solution.py:32
  439.3 47.4 %collective-permute-start.27 = (f32[8,8,8,128]{3,2,1,0:T(8,128)S(1)}, f32[8,8,8,128]{3,2,1,0:T(8,128)S(1)}, u32[]{:S(2)}, u32[]{:S(2)}) collective-permute-start(f32[8,8,8,128]{3,2,1,0:T(8,128)S(1)} %bitcast.241), channel_id=1, source_target_pairs={{0,12},{1,13},{2,14},{3,15},{4,0},{5,1},{6,2},{7,3},{8,4},{9,5},{1... | collective-permute-start | bytes 786440 | tf_op jit(solution)/shard_map/ppermute | solution.py:32
  464.8 22.6 %collective-permute-start.28 = (f32[8,8,8,128]{3,2,1,0:T(8,128)S(1)}, f32[8,8,8,128]{3,2,1,0:T(8,128)S(1)}, u32[]{:S(2)}, u32[]{:S(2)}) collective-permute-start(f32[8,8,8,128]{3,2,1,0:T(8,128)S(1)} %bitcast.240), channel_id=1, source_target_pairs={{0,13},{1,14},{2,15},{3,0},{4,1},{5,2},{6,3},{7,4},{8,5},{9,6},{10... | collective-permute-start | bytes 786440 | tf_op jit(solution)/shard_map/ppermute | solution.py:32
  467.4 20.7 %collective-permute-start.29 = (f32[8,8,8,128]{3,2,1,0:T(8,128)S(1)}, f32[8,8,8,128]{3,2,1,0:T(8,128)S(1)}, u32[]{:S(2)}, u32[]{:S(2)}) collective-permute-start(f32[8,8,8,128]{3,2,1,0:T(8,128)S(1)} %bitcast.239), channel_id=1, source_target_pairs={{0,14},{1,15},{2,0},{3,1},{4,2},{5,3},{6,4},{7,5},{8,6},{9,7},{10,... | collective-permute-start | bytes 786440 | tf_op jit(solution)/shard_map/ppermute | solution.py:32
  470.0 18.9 %collective-permute-start.30 = (f32[8,8,8,128]{3,2,1,0:T(8,128)S(1)}, f32[8,8,8,128]{3,2,1,0:T(8,128)S(1)}, u32[]{:S(2)}, u32[]{:S(2)}) collective-permute-start(f32[8,8,8,128]{3,2,1,0:T(8,128)S(1)} %bitcast.238), channel_id=1, source_target_pairs={{0,15},{1,0},{2,1},{3,2},{4,3},{5,4},{6,5},{7,6},{8,7},{9,8},{10,9... | collective-permute-start | bytes 786440 | tf_op jit(solution)/shard_map/ppermute | solution.py:32
  504.3 24.5 %collective-permute-start.31 = (f32[2,8,128,128]{3,2,1,0:T(8,128)S(1)}, f32[2,8,128,128]{3,2,1,0:T(8,128)S(1)}, u32[]{:S(2)}, u32[]{:S(2)}) collective-permute-start(f32[2,8,128,128]{3,2,1,0:T(8,128)S(1)} %get-tuple-element.2), channel_id=1, source_target_pairs={{16,0},{0,16},{17,1},{1,17},{18,2},{2,18},{19,3},{3,19},{20,4},{4,... | collective-permute-start | bytes 3145736 | tf_op jit(solution)/shard_map/ppermute | solution.py:67
  (12 other events, 103.7 us)
